TPU v7x, 32 devices: a whole 2x2x4 slice. The times are simulated.
32 devices in a mesh: group: 4 (over x, core), head: 8 (over z, y).
Axes of the slice: x: 2, y: 2, z: 4, core: 2. Of those that a mesh axis runs over, the one named last changes fastest.
Arguments:
- qkv: bfloat16 [2048, 3, 512], P(('group', 'head')), may hold values from -40 to 40
- pattern: int32 [4, 3, 8, 6], P('group'), may hold values from 0 to 7, as said below
- counts: int32 [4, 3, 8], P('group'), may hold values from 0 to 6, as said below
Outputs:
- attended: bfloat16 [2048, 512], P(('group', 'head'))
Inputs may be any that keep to these rules, and one draw needn't show every extreme that they name: `pattern`: within one list (g, j, n) the 6 blocks are distinct; at offset index 1 the first entry of query block n's list is n. `counts`: at offset index 1 every count is 1 or more; some count equals 6.
All inputs are finite; a program needn't handle non-finite values.
Results may differ from a plain program's by a relative error of at most 0.0044.
Values may be sent and summed in bfloat16 or wider, within the bound.
No kernel may reach another device: no remote copies, remote signals or barrier semaphores. Data moves between devices by JAX's collectives and lax.ppermute only.
A program may use at most 64 MiB of HBM per device.

v0:
```python
import jax
import jax.numpy as jnp
from jax import lax
from jax.sharding import PartitionSpec as P

BLOCK = 64


def from_behind(value, axis, steps):
    count = lax.axis_size(axis)
    pairs = [(source, (source + steps) % count) for source in range(count)]
    return lax.ppermute(value, axis, pairs)


def body(qkv, pattern, counts):
    half = lax.axis_size("group") // 4
    gathered = lax.all_to_all(qkv, "head", split_axis=2, concat_axis=0, tiled=True)
    group_rows = gathered.shape[0]
    head_dim = gathered.shape[2]
    blocks = group_rows // BLOCK
    query = gathered[:, 0].reshape(blocks, BLOCK, head_dim)
    paired = jnp.concatenate([gathered[:, 1], gathered[:, 2]], axis=-1)
    lists = pattern[0]
    live_counts = counts[0]
    scale = head_dim ** (-0.5)

    def attend(state, source, offset, keep):
        chosen = lax.dynamic_index_in_dim(lists, offset, 0, keepdims=False)
        number = lax.dynamic_index_in_dim(live_counts, offset, 0, keepdims=False) * keep
        width = chosen.shape[1]
        tiles = source.reshape(blocks, BLOCK, 2 * head_dim)[chosen]
        tiles = tiles.reshape(blocks, width * BLOCK, 2 * head_dim)
        key_part = tiles[..., :head_dim]
        value_part = tiles[..., head_dim:]
        scores = (
            jnp.einsum("nqd,nkd->nqk", query, key_part, preferred_element_type=jnp.float32) * scale
        )
        live = (jnp.arange(width * BLOCK, dtype=jnp.int32) // BLOCK)[None, :] < number[:, None]
        scores = jnp.where(live[:, None, :], scores, -jnp.inf)
        running, total, accum = state
        newmax = jnp.maximum(running, scores.max(axis=-1))
        weights = jnp.exp(scores - newmax[..., None])
        factor = jnp.exp(running - newmax)
        total = total * factor + weights.sum(axis=-1)
        accum = accum * factor[..., None] + jnp.einsum(
            "nqk,nkd->nqd",
            weights.astype(jnp.bfloat16),
            value_part,
            preferred_element_type=jnp.float32,
        )
        return (newmax, total, accum)

    start = (
        jnp.full((blocks, BLOCK), -jnp.inf, jnp.float32),
        jnp.zeros((blocks, BLOCK), jnp.float32),
        jnp.zeros((blocks, BLOCK, head_dim), jnp.float32),
    )
    state = attend(start, paired, half, jnp.int32(1))

    def both_step(step_index, carry):
        ahead, behind, state = carry
        ahead = from_behind(ahead, "group", 1)
        behind = from_behind(behind, "group", -1)
        state = attend(state, ahead, half - step_index, jnp.int32(1))
        state = attend(state, behind, half + step_index, jnp.int32(1))
        return (ahead, behind, state)

    ahead, behind, state = lax.fori_loop(1, half + 1, both_step, (paired, paired, state))
    running, total, accum = state
    output = (accum / total[..., None]).astype(jnp.bfloat16).reshape(group_rows, head_dim)
    return lax.all_to_all(output, "head", split_axis=0, concat_axis=1, tiled=True)


def solution(mesh):
    return jax.shard_map(
        body,
        mesh=mesh,
        in_specs=(
            P(("group", "head"), None, None),
            P("group", None, None, None),
            P("group", None, None),
        ),
        out_specs=P(("group", "head"), None),
        check_vma=False,
    )
```

profile of v0, /device:TPU:0, one launch (start us, length us, event | category | flops | bytes accessed | tf_op | source)
XLA Modules:
  0.0 40.3 jit_solution(15031859175372729375)
XLA Ops:
  0.0 1.2 %copy.19 = bf16[64,3,512]{0,1,2:T(4,128)(2,1)S(1)} copy(bf16[64,3,512]{2,0,1:T(8,128)(2,1)} %param.3) | data formatting | bytes 393216 | tf_op args[0]
  1.2 1.0 %reshape.303 = bf16[8,2,6144]{2,1,0:T(2,128)(2,1)} reshape(bf16[512,3,64]{2,1,0:T(4,128)(2,1)S(1)} %bitcast.55) | data formatting | bytes 393216
  2.3 7.4 %all-to-all-start = ((bf16[8,2,6144]{2,1,0:T(2,128)(2,1)}), bf16[8,2,6144]{2,1,0:T(2,128)(2,1)S(1)}, u32[]{:S(2)}, u32[]{:S(2)}) async-start(bf16[8,2,6144]{2,1,0:T(2,128)(2,1)} %reshape.303), calls=%async_computation | async-start | bytes 393216 | tf_op jit(solution)/shard_map/all_to_all | solution.py:17
  9.8 0.1 copy.24
  9.8 0.1 reshape.283
  9.9 0.1 copy.21
  10.0 0.1 reshape.275
  10.1 0.1 copy.27
  10.2 0.1 reshape.291
  10.4 7.3 %all-to-all-done = bf16[8,2,6144]{2,1,0:T(2,128)(2,1)S(1)} async-done(((bf16[8,2,6144]{2,1,0:T(2,128)(2,1)}), bf16[8,2,6144]{2,1,0:T(2,128)(2,1)S(1)}, u32[]{:S(2)}, u32[]{:S(2)}) %all-to-all-start) | async-done | bytes 196640 | tf_op jit(solution)/shard_map/all_to_all | solution.py:17
  17.7 0.3 reshape.304
  18.0 0.3 copy.20
  18.4 0.1 pad_maximum_fusion.1
  18.6 0.5 %collective-permute-start = (bf16[512,128]{1,0:T(8,128)(2,1)S(1)}, bf16[512,128]{1,0:T(8,128)(2,1)S(1)}, u32[]{:S(2)}, u32[]{:S(2)}) collective-permute-start(bf16[512,128]{1,0:T(8,128)(2,1)S(1)} %pad_maximum_fusion.1), channel_id=1, source_target_pairs={{0,8},{8,16},{16,24},{24,0},{1,9},{9,17},{17,25},{25,1},{2,10},{10... | collective-permute-start | bytes 393224 | tf_op jit(solution)/shard_map/while/body/eval_jaxpr/ppermute | solution.py:12
  19.1 0.1 pad_maximum_fusion
  19.2 0.7 %gather_fusion = bf16[48,64,128]{2,1,0:T(8,128)(2,1)S(1)} fusion(bf16[8,64,128]{2,1,0:T(8,128)(2,1)S(1)} %pad_maximum_fusion, s32[1024]{0:T(1024)S(1)} %pad_clamp_fusion.2), kind=kCustom, calls=%fused_computation | custom fusion | bytes 1573056 | tf_op jit(solution)/shard_map/gather | solution.py:31
  19.9 0.5 %fusion.32 = (f32[8,64]{1,0:T(8,128)S(1)}, f32[8,64,384]{2,1,0:T(8,128)S(1)}) fusion(bf16[8,64,64]{2,1,0:T(8,128)(2,1)S(1)} %bitcast.56, bf16[8,384,128]{2,1,0:T(8,128)(2,1)S(1)} %bitcast.46, pred[8,384]{1,0:T(8,128)(4,1)S(1)} %get-tuple-element.51), kind=kOutput, calls=%fused_computation.65 | convolution fusion | flops 25755136 | bytes 1643520 | tf_op jit(solution)/shard_map/nqd,nkd->nqk/dot_general | solution.py:36
  20.4 0.3 fusion.16
  20.8 3.7 %collective-permute-done = bf16[512,128]{1,0:T(8,128)(2,1)S(1)} collective-permute-done((bf16[512,128]{1,0:T(8,128)(2,1)S(1)}, bf16[512,128]{1,0:T(8,128)(2,1)S(1)}, u32[]{:S(2)}, u32[]{:S(2)}) %collective-permute-start) | collective-permute-done | bytes 131104 | tf_op jit(solution)/shard_map/while/body/eval_jaxpr/ppermute | solution.py:12
  24.4 0.7 %gather_fusion.1 = bf16[48,64,128]{2,1,0:T(8,128)(2,1)S(1)} fusion(bf16[8,64,128]{2,1,0:T(8,128)(2,1)S(1)} %bitcast.51, s32[1024]{0:T(1024)S(1)} %pad_clamp_fusion.1), kind=kCustom, calls=%fused_computation.1 | custom fusion | bytes 1573056 | tf_op jit(solution)/shard_map/while/body/eval_jaxpr/gather | solution.py:31
  25.1 0.7 %gather_fusion.2 = bf16[48,64,128]{2,1,0:T(8,128)(2,1)S(1)} fusion(bf16[8,64,128]{2,1,0:T(8,128)(2,1)S(1)} %bitcast.50, s32[1024]{0:T(1024)S(1)} %pad_clamp_fusion), kind=kCustom, calls=%fused_computation.2 | custom fusion | bytes 1573056 | tf_op jit(solution)/shard_map/while/body/eval_jaxpr/gather | solution.py:31
  25.8 0.5 %fusion.33 = (f32[8,64]{1,0:T(8,128)S(1)}, f32[8,64,384]{2,1,0:T(8,128)S(1)}) fusion(bf16[8,64,64]{2,1,0:T(8,128)(2,1)S(1)} %bitcast.57, bf16[8,384,128]{2,1,0:T(8,128)(2,1)S(1)} %bitcast.52, pred[8,384]{1,0:T(8,128)(4,1)S(1)} %get-tuple-element.50), kind=kOutput, calls=%fused_computation.66 | convolution fusion | flops 25755136 | bytes 1643520 | tf_op jit(solution)/shard_map/while/body/eval_jaxpr/nqd,nkd->nqk/dot_general | solution.py:36
  26.4 0.5 %fusion.34 = (f32[8,64]{1,0:T(8,128)S(1)}, f32[8,64,384]{2,1,0:T(8,128)S(1)}) fusion(bf16[8,64,64]{2,1,0:T(8,128)(2,1)S(1)} %bitcast.58, bf16[8,384,128]{2,1,0:T(8,128)(2,1)S(1)} %bitcast.48, pred[8,384]{1,0:T(8,128)(4,1)S(1)} %get-tuple-element.49), kind=kOutput, calls=%fused_computation.67 | convolution fusion | flops 25755136 | bytes 1643520 | tf_op jit(solution)/shard_map/while/body/eval_jaxpr/nqd,nkd->nqk/dot_general | solution.py:36
  26.9 0.5 %fusion.18 = (f32[8,64]{1,0:T(8,128)S(1)}, f32[8,64]{1,0:T(8,128)S(1)}) fusion(f32[8,64,384]{2,1,0:T(8,128)S(1)} %get-tuple-element.60, f32[8,64]{1,0:T(8,128)S(1)} %get-tuple-element.27, f32[8,64,384]{2,1,0:T(8,128)S(1)} %get-tuple-element.58, f32[8,64]{1,0:T(8,128)S(1)} %get-tuple-element.26), kind=kLoop, calls=%fused_computation.30 | loop fusion | flops 785408 | bytes 1581056 | tf_op jit(solution)/shard_map/while/body/eval_jaxpr/reduce_sum | solution.py:44
  27.5 0.6 %fusion.8 = f32[8,64,64]{2,1,0:T(8,128)S(1)} fusion(bf16[8,384,128]{2,1,0:T(8,128)(2,1)S(1)} %bitcast.47, f32[8,64,384]{2,1,0:T(8,128)S(1)} %get-tuple-element.56, f32[8,64]{1,0:T(8,128)S(1)} %get-tuple-element.55, f32[8,64]{1,0:T(8,128)S(1)} %get-tuple-element.25, f32[8,64]{1,0:T(8,128)S(1)} %get-tuple-element.48), kind=kOutput, calls=%fused_computation.17 | convolution fusion | flops 25624576 | bytes 1710080 | tf_op jit(solution)/shard_map/nqk,nkd->nqd/dot_general | solution.py:45
  28.1 0.6 %fusion.7 = f32[8,64,64]{2,1,0:T(8,128)S(1)} fusion(f32[8,64,64]{2,1,0:T(8,128)S(1)} %fusion.8, bf16[8,384,128]{2,1,0:T(8,128)(2,1)S(1)} %bitcast.49, f32[8,64,384]{2,1,0:T(8,128)S(1)} %get-tuple-element.60, f32[8,64]{1,0:T(8,128)S(1)} %get-tuple-element.27, f32[8,64]{1,0:T(8,128)S(1)} %get-tuple-element.24), kind=kOutput, calls=%fused_computation.15 | convolution fusion | flops 25624576 | bytes 1839104 | tf_op jit(solution)/shard_map/while/body/eval_jaxpr/nqk,nkd->nqd/dot_general | solution.py:45
  28.7 0.6 %fusion.9 = bf16[8,64,64]{2,1,0:T(8,128)(2,1)S(1)} fusion(f32[8,64,64]{2,1,0:T(8,128)S(1)} %fusion.7, bf16[8,384,128]{2,1,0:T(8,128)(2,1)S(1)} %bitcast.53, f32[8,64,384]{2,1,0:T(8,128)S(1)} %get-tuple-element.58, f32[8,64]{1,0:T(8,128)S(1)} %get-tuple-element.26, f32[8,64]{1,0:T(8,128)S(1)} %get-tuple-element.23), kind=kOutput, calls=%fused_computation.18 | convolution fusion | flops 25657344 | bytes 1773568 | tf_op jit(solution)/shard_map/while/body/eval_jaxpr/nqk,nkd->nqd/dot_general | solution.py:45
  29.2 0.2 reshape.305
  29.4 9.8 %all_to_all.34 = bf16[8,2,2048]{2,1,0:T(2,128)(2,1)S(1)} all-to-all(bf16[8,2,2048]{2,1,0:T(2,128)(2,1)S(1)} %reshape.305), channel_id=1, replica_groups=mesh['group'=4,'head'=8] {'head'}, dimensions={0} | all-to-all | bytes 131072 | tf_op jit(solution)/shard_map/all_to_all | solution.py:71
  39.2 0.1 reshape.306
  39.4 0.1 copy.30
  39.5 0.8 %all_to_all.31 = bf16[64,512]{1,0:T(8,128)(2,1)} reshape(bf16[64,8,64]{2,1,0:T(8,128)(2,1)S(1)} %copy.30) | data formatting | bytes 131072 | tf_op jit(solution)/shard_map/all_to_all | solution.py:71
  (16 shorter events, 0.3 us)
Async XLA Ops:
  2.3 7.4 %copy-start.1 = (s32[1,3,8]{2,0,1:T(1,128)S(1)}, s32[1,3,8]{2,0,1:T(1,128)}, u32[]{:S(2)}) copy-start(s32[1,3,8]{2,0,1:T(1,128)} %param.5) | copy-start | bytes 292
  2.3 7.5 %copy-start = (s32[1,3,8,6]{2,0,3,1:T(1,128)S(1)}, s32[1,3,8,6]{2,0,3,1:T(1,128)}, u32[]{:S(2)}) copy-start(s32[1,3,8,6]{2,0,3,1:T(1,128)} %param.4) | copy-start | bytes 1732
  2.3 15.4 %all-to-all-start = ((bf16[8,2,6144]{2,1,0:T(2,128)(2,1)}), bf16[8,2,6144]{2,1,0:T(2,128)(2,1)S(1)}, u32[]{:S(2)}, u32[]{:S(2)}) async-start(bf16[8,2,6144]{2,1,0:T(2,128)(2,1)} %reshape.303), calls=%async_computation | async-start | bytes 393216 | tf_op jit(solution)/shard_map/all_to_all | solution.py:17
  18.5 6.6 %collective-permute-start.1 = (bf16[512,128]{1,0:T(8,128)(2,1)S(1)}, bf16[512,128]{1,0:T(8,128)(2,1)S(1)}, u32[]{:S(2)}, u32[]{:S(2)}) collective-permute-start(bf16[512,128]{1,0:T(8,128)(2,1)S(1)} %pad_maximum_fusion.1), channel_id=1, source_target_pairs={{0,24},{8,0},{16,8},{24,16},{1,25},{9,1},{17,9},{25,17},{2,26},{10... | collective-permute-start | bytes 393224 | tf_op jit(solution)/shard_map/while/body/eval_jaxpr/ppermute | solution.py:12
  18.6 5.8 %collective-permute-start = (bf16[512,128]{1,0:T(8,128)(2,1)S(1)}, bf16[512,128]{1,0:T(8,128)(2,1)S(1)}, u32[]{:S(2)}, u32[]{:S(2)}) collective-permute-start(bf16[512,128]{1,0:T(8,128)(2,1)S(1)} %pad_maximum_fusion.1), channel_id=1, source_target_pairs={{0,8},{8,16},{16,24},{24,0},{1,9},{9,17},{17,25},{25,1},{2,10},{10... | collective-permute-start | bytes 393224 | tf_op jit(solution)/shard_map/while/body/eval_jaxpr/ppermute | solution.py:12
where the time goes:
time: 40.6 us; the launch traced here: 40.3 us
  waiting for transfers between devices  11 us (27%)
  blocking collectives  9.85 us (24%)
  starting transfers between devices  7.99 us (20%)
  local copies, waits for them, and re-layouts  6.72 us (17%)
  matrix products  3.38 us (8%)
  other arithmetic  1.19 us (3%)
    all_to_all x1, blocking collectives, body(): lax.all_to_all(output, 'head', split_axis=0, concat_axis=1, tiled=True)  9.85 us
    all_to_all x1, starting transfers between devices, body(): lax.all_to_all(qkv, 'head', split_axis=2, concat_axis=0, tiled=True)  7.44 us
    all_to_all x1, waiting for transfers between devices, body(): lax.all_to_all(qkv, 'head', split_axis=2, concat_axis=0, tiled=True)  7.3 us
    ppermute x2, waiting for transfers between devices, from_behind(): return lax.ppermute(value, axis, pairs)  3.65 us
    unnamed x9, local copies, waits for them, and re-layouts  2.87 us
    gather x3, local copies, waits for them, and re-layouts, attend(): tiles = source.reshape(blocks, BLOCK, 2 * head_dim)[chosen]  2.09 us
    dot_general x3, matrix products, attend(): jnp.einsum('nqk,nkd->nqd', weights.astype(jnp.bfloat16), value_part, pref...  1.75 us
    dot_general x3, matrix products, attend(): jnp.einsum('nqd,nkd->nqk', query, key_part, preferred_element_type=jnp.fl...  1.63 us
  transfers between devices with their start and end apart: 3, of which 2 were waited for; matrix products, arithmetic and copies ran while one was open for 7% of the time, Pallas kernels for 0%

commit v1 on v0

--- a/solution.py
+++ b/solution.py
@@ -4,6 +4,17 @@
 from jax.sharding import PartitionSpec as P
 
 BLOCK = 64
+
+
+def in_blocks(x, dim, length):
+    before, after = (x.shape[:dim], x.shape[dim + 1 :])
+    return jnp.moveaxis(x.reshape(*before, length, -1, *after), dim, 0)
+
+
+def laid_out(blocks, dim):
+    blocks = jnp.moveaxis(blocks, 0, dim)
+    dims = blocks.shape
+    return blocks.reshape(*dims[:dim], dims[dim] * dims[dim + 1], *dims[dim + 2 :])
 
 
 def from_behind(value, axis, steps):
@@ -14,7 +25,14 @@
 
 def body(qkv, pattern, counts):
     half = lax.axis_size("group") // 4
-    gathered = lax.all_to_all(qkv, "head", split_axis=2, concat_axis=0, tiled=True)
+    count_2, index = (lax.axis_size("head"), lax.axis_index("head"))
+    pieces = in_blocks(qkv, 2, count_2)
+    outs = [pieces[index]]
+    for step in range(1, count_2):
+        sent = pieces[index ^ step]
+        outs.append(lax.ppermute(sent, "head", [(i, i ^ step) for i in range(count_2)]))
+    pieces = jnp.stack(outs)[index ^ jnp.arange(count_2)]
+    gathered = laid_out(pieces, 0)
     group_rows = gathered.shape[0]
     head_dim = gathered.shape[2]
     blocks = group_rows // BLOCK

time: 40.6 us -> 45.5 us (1.12)
  starting transfers between devices: 7.99 us -> 13.9 us
  waiting for transfers between devices: 11 us -> 9.51 us
  local copies, waits for them, and re-layouts: 6.72 us -> 7.76 us
  blocking collectives: 9.85 us -> 9.29 us
    ppermute x0 -> x7, starting transfers between devices: none -> 13.3 us  [body(): lax.ppermute(sent, 'head', [(i, i ^ step) for i in range(count_2)])]
    all_to_all x1 -> x0, starting transfers between devices: 7.44 us -> none  [body(): lax.all_to_all(qkv, 'head', split_axis=2, concat_axis=0, tiled=True)]
    all_to_all x1 -> x0, waiting for transfers between devices: 7.3 us -> none  [body(): lax.all_to_all(qkv, 'head', split_axis=2, concat_axis=0, tiled=True)]
    ppermute x0 -> x7, waiting for transfers between devices: none -> 6.25 us  [body(): lax.ppermute(sent, 'head', [(i, i ^ step) for i in range(count_2)])]
    unnamed x9 -> x20, local copies, waits for them, and re-layouts: 2.87 us -> 0.45 us
    reshape x0 -> x2, local copies, waits for them, and re-layouts: none -> 1.43 us  [the longest x1 1.17 us: in_blocks(): return jnp.moveaxis(x.reshape(*before, length, -1, *after), dim, 0)]
    another operation x0 -> x2, local copies, waits for them, and re-layouts: none -> 0.91 us
    gather x0 -> x2, local copies, waits for them, and re-layouts: none -> 0.88 us  [body(): pieces = jnp.stack(outs)[index ^ jnp.arange(count_2)]]
  transfers between devices with their start and end apart: 3 -> 9, of which waited for: 2 -> 4; matrix products, arithmetic and copies ran while one was open for 7% -> 8% of each run, Pallas kernels for 0% -> 0%
where the time goes in v1:
time: 45.5 us; the launch traced here: 45.3 us
  starting transfers between devices  13.9 us (31%)
  waiting for transfers between devices  9.51 us (21%)
  blocking collectives  9.29 us (20%)
  local copies, waits for them, and re-layouts  7.76 us (17%)
  matrix products  3.4 us (7%)
  other arithmetic  1.1 us (2%)
    ppermute x7, starting transfers between devices, body(): lax.ppermute(sent, 'head', [(i, i ^ step) for i in range(count_2)])  13.3 us
    all_to_all x1, blocking collectives, body(): lax.all_to_all(output, 'head', split_axis=0, concat_axis=1, tiled=True)  9.29 us
    ppermute x7, waiting for transfers between devices, body(): lax.ppermute(sent, 'head', [(i, i ^ step) for i in range(count_2)])  6.25 us
    ppermute x2, waiting for transfers between devices, from_behind(): return lax.ppermute(value, axis, pairs)  3.27 us
    gather x3, local copies, waits for them, and re-layouts, attend(): tiles = source.reshape(blocks, BLOCK, 2 * head_dim)[chosen]  2.1 us
    dot_general x3, matrix products, attend(): jnp.einsum('nqk,nkd->nqd', weights.astype(jnp.bfloat16), value_part, pref...  1.75 us
    dot_general x3, matrix products, attend(): jnp.einsum('nqd,nkd->nqk', query, key_part, preferred_element_type=jnp.fl...  1.64 us
    reshape x1, local copies, waits for them, and re-layouts, in_blocks(): return jnp.moveaxis(x.reshape(*before, length, -1, *after), dim, 0)  1.17 us
  transfers between devices with their start and end apart: 9, of which 4 were waited for; matrix products, arithmetic and copies ran while one was open for 8% of the time, Pallas kernels for 0%

profile of v1, /device:TPU:0, one launch (start us, length us, event | category | flops | bytes accessed | tf_op | source)
XLA Modules:
  0.0 45.3 jit_solution(12771732293963914813)
XLA Ops:
  0.0 1.2 %reshape.305 = bf16[64,3,8,64]{3,2,0,1:T(8,128)(2,1)S(1)} reshape(bf16[64,3,512]{2,0,1:T(8,128)(2,1)} %param.3) | data formatting | bytes 393216 | tf_op jit(solution)/shard_map/reshape | solution.py:11
  1.2 0.9 %constant_dynamic-slice_fusion = (bf16[64,3,1,64]{3,2,0,1:T(2,128)(2,1)S(1)}, bf16[64,3,1,64]{3,2,0,1:T(2,128)(2,1)S(1)}, bf16[64,3,1,64]{3,2,0,1:T(2,128)(2,1)S...) fusion(bf16[64,3,8,64]{3,2,0,1:T(8,128)(2,1)S(1)} %reshape.305,, ...), kind=kLoop, calls=%fused_computation.73 | loop fusion | bytes 393248 | tf_op jit(solution)/shard_map/dynamic-slice.8
  2.1 3.1 %collective-permute-start = (bf16[64,3,64]{2,0,1:T(8,128)(2,1)S(1)}, bf16[64,3,64]{2,0,1:T(8,128)(2,1)S(1)}, u32[]{:S(2)}, u32[]{:S(2)}) collective-permute-start(bf16[64,3,64]{2,0,1:T(8,128)(2,1)S(1)} %bitcast.97), channel_id=1, source_target_pairs={{0,1},{1,0},{2,3},{3,2},{4,5},{5,4},{6,7},{7,6},{8,9},{9,8},{10,11... | collective-permute-start | bytes 73736 | tf_op jit(solution)/shard_map/ppermute | solution.py:33
  5.2 1.6 %collective-permute-start.1 = (bf16[64,3,64]{2,0,1:T(8,128)(2,1)S(1)}, bf16[64,3,64]{2,0,1:T(8,128)(2,1)S(1)}, u32[]{:S(2)}, u32[]{:S(2)}) collective-permute-start(bf16[64,3,64]{2,0,1:T(8,128)(2,1)S(1)} %bitcast.96), channel_id=1, source_target_pairs={{0,2},{1,3},{2,0},{3,1},{4,6},{5,7},{6,4},{7,5},{8,10},{9,11},{10,... | collective-permute-start | bytes 73736 | tf_op jit(solution)/shard_map/ppermute | solution.py:33
  7.0 3.0 %collective-permute-start.3 = (bf16[64,3,64]{2,0,1:T(8,128)(2,1)S(1)}, bf16[64,3,64]{2,0,1:T(8,128)(2,1)S(1)}, u32[]{:S(2)}, u32[]{:S(2)}) collective-permute-start(bf16[64,3,64]{2,0,1:T(8,128)(2,1)S(1)} %bitcast.94), channel_id=1, source_target_pairs={{0,4},{1,5},{2,6},{3,7},{4,0},{5,1},{6,2},{7,3},{8,12},{9,13},{10,... | collective-permute-start | bytes 73736 | tf_op jit(solution)/shard_map/ppermute | solution.py:33
  10.0 1.4 %collective-permute-start.4 = (bf16[64,3,64]{2,0,1:T(8,128)(2,1)S(1)}, bf16[64,3,64]{2,0,1:T(8,128)(2,1)S(1)}, u32[]{:S(2)}, u32[]{:S(2)}) collective-permute-start(bf16[64,3,64]{2,0,1:T(8,128)(2,1)S(1)} %bitcast.93), channel_id=1, source_target_pairs={{0,5},{1,4},{2,7},{3,6},{4,1},{5,0},{6,3},{7,2},{8,13},{9,12},{10,... | collective-permute-start | bytes 73736 | tf_op jit(solution)/shard_map/ppermute | solution.py:33
  12.1 3.7 %collective-permute-start.5 = (bf16[64,3,64]{2,0,1:T(8,128)(2,1)S(1)}, bf16[64,3,64]{2,0,1:T(8,128)(2,1)S(1)}, u32[]{:S(2)}, u32[]{:S(2)}) collective-permute-start(bf16[64,3,64]{2,0,1:T(8,128)(2,1)S(1)} %bitcast.99), channel_id=1, source_target_pairs={{0,6},{1,7},{2,4},{3,5},{4,2},{5,3},{6,0},{7,1},{8,14},{9,15},{10,... | collective-permute-start | bytes 73736 | tf_op jit(solution)/shard_map/ppermute | solution.py:33
  15.8 0.5 %collective-permute-start.6 = (bf16[64,3,64]{2,0,1:T(8,128)(2,1)S(1)}, bf16[64,3,64]{2,0,1:T(8,128)(2,1)S(1)}, u32[]{:S(2)}, u32[]{:S(2)}) collective-permute-start(bf16[64,3,64]{2,0,1:T(8,128)(2,1)S(1)} %bitcast.98), channel_id=1, source_target_pairs={{0,7},{1,6},{2,5},{3,4},{4,3},{5,2},{6,1},{7,0},{8,15},{9,14},{10,... | collective-permute-start | bytes 73736 | tf_op jit(solution)/shard_map/ppermute | solution.py:33
  16.4 0.8 %collective-permute-done.4 = bf16[64,3,64]{2,0,1:T(8,128)(2,1)S(1)} collective-permute-done((bf16[64,3,64]{2,0,1:T(8,128)(2,1)S(1)}, bf16[64,3,64]{2,0,1:T(8,128)(2,1)S(1)}, u32[]{:S(2)}, u32[]{:S(2)}) %collective-permute-start.4) | collective-permute-done | bytes 24608 | tf_op jit(solution)/shard_map/ppermute | solution.py:33
  17.2 0.8 %collective-permute-done.5 = bf16[64,3,64]{2,0,1:T(8,128)(2,1)S(1)} collective-permute-done((bf16[64,3,64]{2,0,1:T(8,128)(2,1)S(1)}, bf16[64,3,64]{2,0,1:T(8,128)(2,1)S(1)}, u32[]{:S(2)}, u32[]{:S(2)}) %collective-permute-start.5) | collective-permute-done | bytes 24608 | tf_op jit(solution)/shard_map/ppermute | solution.py:33
  18.1 4.6 %collective-permute-done.6 = bf16[64,3,64]{2,0,1:T(8,128)(2,1)S(1)} collective-permute-done((bf16[64,3,64]{2,0,1:T(8,128)(2,1)S(1)}, bf16[64,3,64]{2,0,1:T(8,128)(2,1)S(1)}, u32[]{:S(2)}, u32[]{:S(2)}) %collective-permute-start.6) | collective-permute-done | bytes 24608 | tf_op jit(solution)/shard_map/ppermute | solution.py:33
  22.7 0.6 %gather_fusion = bf16[8,64,3,64]{3,1,2,0:T(8,128)(2,1)S(1)} fusion(bf16[8,64,3,64]{3,1,2,0:T(8,128)(2,1)S(1)} %bitcast_dynamic-update-slice_fusion.1, s32[1024]{0:T(1024)S(1)} %pad_clamp_fusion.3), kind=kCustom, calls=%fused_computation | custom fusion | bytes 393248 | tf_op jit(solution)/shard_map/gather | solution.py:34
  23.3 0.3 copy.29
  23.6 0.3 reshape.306
  23.9 0.5 %collective-permute-start.7 = (bf16[512,128]{0,1:T(8,128)(2,1)S(1)}, bf16[512,128]{0,1:T(8,128)(2,1)S(1)}, u32[]{:S(2)}, u32[]{:S(2)}) collective-permute-start(bf16[512,128]{0,1:T(8,128)(2,1)S(1)} %pad_maximum_fusion.1), channel_id=1, source_target_pairs={{0,8},{8,16},{16,24},{24,0},{1,9},{9,17},{17,25},{25,1},{2,10},{10... | collective-permute-start | bytes 393224 | tf_op jit(solution)/shard_map/while/body/eval_jaxpr/ppermute | solution.py:23
  24.6 0.1 copy.31
  24.9 0.7 %gather_fusion.1 = bf16[48,64,128]{2,1,0:T(8,128)(2,1)S(1)} fusion(bf16[8,64,128]{2,1,0:T(8,128)(2,1)S(1)} %pad_maximum_fusion, s32[1024]{0:T(1024)S(1)} %pad_clamp_fusion.2), kind=kCustom, calls=%fused_computation.1 | custom fusion | bytes 1573056 | tf_op jit(solution)/shard_map/gather | solution.py:49
  25.6 0.5 %fusion.30 = (f32[8,64]{1,0:T(8,128)S(1)}, f32[8,64,384]{2,1,0:T(8,128)S(1)}) fusion(bf16[8,64,64]{2,1,0:T(8,128)(2,1)S(1)} %bitcast.87, bf16[8,384,128]{2,1,0:T(8,128)(2,1)S(1)} %bitcast.79, pred[8,384]{1,0:T(8,128)(4,1)S(1)} %get-tuple-element.59), kind=kOutput, calls=%fused_computation.89 | convolution fusion | flops 25755136 | bytes 1643520 | tf_op jit(solution)/shard_map/nqd,nkd->nqk/dot_general | solution.py:54
  26.2 0.3 fusion.13
  26.5 3.3 %collective-permute-done.7 = bf16[512,128]{0,1:T(8,128)(2,1)S(1)} collective-permute-done((bf16[512,128]{0,1:T(8,128)(2,1)S(1)}, bf16[512,128]{0,1:T(8,128)(2,1)S(1)}, u32[]{:S(2)}, u32[]{:S(2)}) %collective-permute-start.7) | collective-permute-done | bytes 131104 | tf_op jit(solution)/shard_map/while/body/eval_jaxpr/ppermute | solution.py:23
  29.9 0.7 %gather_fusion.2 = bf16[48,64,128]{2,1,0:T(8,128)(2,1)S(1)} fusion(bf16[8,64,128]{2,1,0:T(8,128)(2,1)S(1)} %bitcast.83, s32[1024]{0:T(1024)S(1)} %pad_clamp_fusion.1), kind=kCustom, calls=%fused_computation.2 | custom fusion | bytes 1573056 | tf_op jit(solution)/shard_map/while/body/eval_jaxpr/gather | solution.py:49
  30.7 0.7 %gather_fusion.3 = bf16[48,64,128]{2,1,0:T(8,128)(2,1)S(1)} fusion(bf16[8,64,128]{2,1,0:T(8,128)(2,1)S(1)} %bitcast.84, s32[1024]{0:T(1024)S(1)} %pad_clamp_fusion), kind=kCustom, calls=%fused_computation.3 | custom fusion | bytes 1573056 | tf_op jit(solution)/shard_map/while/body/eval_jaxpr/gather | solution.py:49
  31.5 0.5 %fusion.31 = (f32[8,64]{1,0:T(8,128)S(1)}, f32[8,64,384]{2,1,0:T(8,128)S(1)}) fusion(bf16[8,64,64]{2,1,0:T(8,128)(2,1)S(1)} %bitcast.88, bf16[8,384,128]{2,1,0:T(8,128)(2,1)S(1)} %bitcast.85, pred[8,384]{1,0:T(8,128)(4,1)S(1)} %get-tuple-element.58), kind=kOutput, calls=%fused_computation.90 | convolution fusion | flops 25755136 | bytes 1643520 | tf_op jit(solution)/shard_map/while/body/eval_jaxpr/nqd,nkd->nqk/dot_general | solution.py:54
  32.0 0.6 %fusion.32 = (f32[8,64]{1,0:T(8,128)S(1)}, f32[8,64,384]{2,1,0:T(8,128)S(1)}) fusion(bf16[8,64,64]{2,1,0:T(8,128)(2,1)S(1)} %bitcast.89, bf16[8,384,128]{2,1,0:T(8,128)(2,1)S(1)} %bitcast.81, pred[8,384]{1,0:T(8,128)(4,1)S(1)} %get-tuple-element.57), kind=kOutput, calls=%fused_computation.91 | convolution fusion | flops 25755136 | bytes 1643520 | tf_op jit(solution)/shard_map/while/body/eval_jaxpr/nqd,nkd->nqk/dot_general | solution.py:54
  32.6 0.5 %fusion.15 = (f32[8,64]{1,0:T(8,128)S(1)}, f32[8,64]{1,0:T(8,128)S(1)}) fusion(f32[8,64,384]{2,1,0:T(8,128)S(1)} %get-tuple-element.68, f32[8,64]{1,0:T(8,128)S(1)} %get-tuple-element.27, f32[8,64,384]{2,1,0:T(8,128)S(1)} %get-tuple-element.66, f32[8,64]{1,0:T(8,128)S(1)} %get-tuple-element.26), kind=kLoop, calls=%fused_computation.28 | loop fusion | flops 785408 | bytes 1581056 | tf_op jit(solution)/shard_map/while/body/eval_jaxpr/reduce_sum | solution.py:62
  33.1 0.6 %fusion.5 = f32[8,64,64]{2,1,0:T(8,128)S(1)} fusion(bf16[8,384,128]{2,1,0:T(8,128)(2,1)S(1)} %bitcast.80, f32[8,64,384]{2,1,0:T(8,128)S(1)} %get-tuple-element.64, f32[8,64]{1,0:T(8,128)S(1)} %get-tuple-element.63, f32[8,64]{1,0:T(8,128)S(1)} %get-tuple-element.25, f32[8,64]{1,0:T(8,128)S(1)} %get-tuple-element.56), kind=kOutput, calls=%fused_computation.15 | convolution fusion | flops 25624576 | bytes 1710080 | tf_op jit(solution)/shard_map/nqk,nkd->nqd/dot_general | solution.py:63
  33.7 0.6 %fusion.4 = f32[8,64,64]{2,1,0:T(8,128)S(1)} fusion(f32[8,64,64]{2,1,0:T(8,128)S(1)} %fusion.5, bf16[8,384,128]{2,1,0:T(8,128)(2,1)S(1)} %bitcast.82, f32[8,64,384]{2,1,0:T(8,128)S(1)} %get-tuple-element.68, f32[8,64]{1,0:T(8,128)S(1)} %get-tuple-element.27, f32[8,64]{1,0:T(8,128)S(1)} %get-tuple-element.24), kind=kOutput, calls=%fused_computation.13 | convolution fusion | flops 25624576 | bytes 1839104 | tf_op jit(solution)/shard_map/while/body/eval_jaxpr/nqk,nkd->nqd/dot_general | solution.py:63
  34.3 0.6 %fusion.6 = bf16[8,64,64]{2,1,0:T(8,128)(2,1)S(1)} fusion(f32[8,64,64]{2,1,0:T(8,128)S(1)} %fusion.4, bf16[8,384,128]{2,1,0:T(8,128)(2,1)S(1)} %bitcast.86, f32[8,64,384]{2,1,0:T(8,128)S(1)} %get-tuple-element.66, f32[8,64]{1,0:T(8,128)S(1)} %get-tuple-element.26, f32[8,64]{1,0:T(8,128)S(1)} %get-tuple-element.23), kind=kOutput, calls=%fused_computation.16 | convolution fusion | flops 25657344 | bytes 1773568 | tf_op jit(solution)/shard_map/while/body/eval_jaxpr/nqk,nkd->nqd/dot_general | solution.py:63
  34.9 0.2 reshape.350
  35.0 9.3 %all_to_all.16 = bf16[8,2,2048]{2,1,0:T(2,128)(2,1)S(1)} all-to-all(bf16[8,2,2048]{2,1,0:T(2,128)(2,1)S(1)} %reshape.350), channel_id=1, replica_groups=mesh['group'=4,'head'=8] {'head'}, dimensions={0} | all-to-all | bytes 131072 | tf_op jit(solution)/shard_map/all_to_all | solution.py:89
  44.3 0.1 reshape.351
  44.6 0.8 %all_to_all.14 = bf16[64,512]{1,0:T(8,128)(2,1)} reshape(bf16[64,8,64]{2,1,0:T(8,128)(2,1)S(1)} %copy.44) | data formatting | bytes 131072 | tf_op jit(solution)/shard_map/all_to_all | solution.py:89
  (51 shorter events, 1.7 us)
Async XLA Ops:
  2.1 10.0 %collective-permute-start = (bf16[64,3,64]{2,0,1:T(8,128)(2,1)S(1)}, bf16[64,3,64]{2,0,1:T(8,128)(2,1)S(1)}, u32[]{:S(2)}, u32[]{:S(2)}) collective-permute-start(bf16[64,3,64]{2,0,1:T(8,128)(2,1)S(1)} %bitcast.97), channel_id=1, source_target_pairs={{0,1},{1,0},{2,3},{3,2},{4,5},{5,4},{6,7},{7,6},{8,9},{9,8},{10,11... | collective-permute-start | bytes 73736 | tf_op jit(solution)/shard_map/ppermute | solution.py:33
  5.2 10.6 %collective-permute-start.1 = (bf16[64,3,64]{2,0,1:T(8,128)(2,1)S(1)}, bf16[64,3,64]{2,0,1:T(8,128)(2,1)S(1)}, u32[]{:S(2)}, u32[]{:S(2)}) collective-permute-start(bf16[64,3,64]{2,0,1:T(8,128)(2,1)S(1)} %bitcast.96), channel_id=1, source_target_pairs={{0,2},{1,3},{2,0},{3,1},{4,6},{5,7},{6,4},{7,5},{8,10},{9,11},{10,... | collective-permute-start | bytes 73736 | tf_op jit(solution)/shard_map/ppermute | solution.py:33
  6.9 9.5 %collective-permute-start.2 = (bf16[64,3,64]{2,0,1:T(8,128)(2,1)S(1)}, bf16[64,3,64]{2,0,1:T(8,128)(2,1)S(1)}, u32[]{:S(2)}, u32[]{:S(2)}) collective-permute-start(bf16[64,3,64]{2,0,1:T(8,128)(2,1)S(1)} %bitcast.95), channel_id=1, source_target_pairs={{0,3},{1,2},{2,1},{3,0},{4,7},{5,6},{6,5},{7,4},{8,11},{9,10},{10,... | collective-permute-start | bytes 73736 | tf_op jit(solution)/shard_map/ppermute | solution.py:33
  7.0 9.4 %collective-permute-start.3 = (bf16[64,3,64]{2,0,1:T(8,128)(2,1)S(1)}, bf16[64,3,64]{2,0,1:T(8,128)(2,1)S(1)}, u32[]{:S(2)}, u32[]{:S(2)}) collective-permute-start(bf16[64,3,64]{2,0,1:T(8,128)(2,1)S(1)} %bitcast.94), channel_id=1, source_target_pairs={{0,4},{1,5},{2,6},{3,7},{4,0},{5,1},{6,2},{7,3},{8,12},{9,13},{10,... | collective-permute-start | bytes 73736 | tf_op jit(solution)/shard_map/ppermute | solution.py:33
  10.0 1.4 %copy-start.1 = (s32[1,3,8]{2,0,1:T(1,128)S(1)}, s32[1,3,8]{2,0,1:T(1,128)}, u32[]{:S(2)}) copy-start(s32[1,3,8]{2,0,1:T(1,128)} %param.5) | copy-start | bytes 292
  10.0 1.4 %copy-start = (s32[1,3,8,6]{2,0,3,1:T(1,128)S(1)}, s32[1,3,8,6]{2,0,3,1:T(1,128)}, u32[]{:S(2)}) copy-start(s32[1,3,8,6]{2,0,3,1:T(1,128)} %param.4) | copy-start | bytes 1732
  10.0 7.2 %collective-permute-start.4 = (bf16[64,3,64]{2,0,1:T(8,128)(2,1)S(1)}, bf16[64,3,64]{2,0,1:T(8,128)(2,1)S(1)}, u32[]{:S(2)}, u32[]{:S(2)}) collective-permute-start(bf16[64,3,64]{2,0,1:T(8,128)(2,1)S(1)} %bitcast.93), channel_id=1, source_target_pairs={{0,5},{1,4},{2,7},{3,6},{4,1},{5,0},{6,3},{7,2},{8,13},{9,12},{10,... | collective-permute-start | bytes 73736 | tf_op jit(solution)/shard_map/ppermute | solution.py:33
  12.1 6.0 %collective-permute-start.5 = (bf16[64,3,64]{2,0,1:T(8,128)(2,1)S(1)}, bf16[64,3,64]{2,0,1:T(8,128)(2,1)S(1)}, u32[]{:S(2)}, u32[]{:S(2)}) collective-permute-start(bf16[64,3,64]{2,0,1:T(8,128)(2,1)S(1)} %bitcast.99), channel_id=1, source_target_pairs={{0,6},{1,7},{2,4},{3,5},{4,2},{5,3},{6,0},{7,1},{8,14},{9,15},{10,... | collective-permute-start | bytes 73736 | tf_op jit(solution)/shard_map/ppermute | solution.py:33
  15.8 6.9 %collective-permute-start.6 = (bf16[64,3,64]{2,0,1:T(8,128)(2,1)S(1)}, bf16[64,3,64]{2,0,1:T(8,128)(2,1)S(1)}, u32[]{:S(2)}, u32[]{:S(2)}) collective-permute-start(bf16[64,3,64]{2,0,1:T(8,128)(2,1)S(1)} %bitcast.98), channel_id=1, source_target_pairs={{0,7},{1,6},{2,5},{3,4},{4,3},{5,2},{6,1},{7,0},{8,15},{9,14},{10,... | collective-permute-start | bytes 73736 | tf_op jit(solution)/shard_map/ppermute | solution.py:33
  23.9 6.7 %collective-permute-start.8 = (bf16[512,128]{0,1:T(8,128)(2,1)S(1)}, bf16[512,128]{0,1:T(8,128)(2,1)S(1)}, u32[]{:S(2)}, u32[]{:S(2)}) collective-permute-start(bf16[512,128]{0,1:T(8,128)(2,1)S(1)} %pad_maximum_fusion.1), channel_id=1, source_target_pairs={{0,24},{8,0},{16,8},{24,16},{1,25},{9,1},{17,9},{25,17},{2,26},{10... | collective-permute-start | bytes 393224 | tf_op jit(solution)/shard_map/while/body/eval_jaxpr/ppermute | solution.py:23
  23.9 5.8 %collective-permute-start.7 = (bf16[512,128]{0,1:T(8,128)(2,1)S(1)}, bf16[512,128]{0,1:T(8,128)(2,1)S(1)}, u32[]{:S(2)}, u32[]{:S(2)}) collective-permute-start(bf16[512,128]{0,1:T(8,128)(2,1)S(1)} %pad_maximum_fusion.1), channel_id=1, source_target_pairs={{0,8},{8,16},{16,24},{24,0},{1,9},{9,17},{17,25},{25,1},{2,10},{10... | collective-permute-start | bytes 393224 | tf_op jit(solution)/shard_map/while/body/eval_jaxpr/ppermute | solution.py:23
